TPU v7x, 128 devices: a whole 4x4x4 slice. The times are simulated.
128 devices in a mesh: wide: 32 (over x, z, core), narrow: 4 (over y).
Axes of the slice: x: 4, y: 4, z: 4, core: 2. Of those that a mesh axis runs over, the one named last changes fastest.
Arguments:
- tokens: bfloat16 [262144, 1024], P(('wide', 'narrow')), may hold values from -64 to 64
- slot_params: bfloat16 [1024, 512], replicated, may hold values from -2.5 to 2.5
- expert_in: bfloat16 [128, 1024, 4096], P('wide', None, 'narrow'), may hold values from -0.1875 to 0.1875
- expert_out: bfloat16 [128, 4096, 1024], P('wide', 'narrow'), may hold values from -0.09375 to 0.09375
Outputs:
- mixed: bfloat16 [262144, 1024], P(('wide', 'narrow'))
All inputs are finite; a program needn't handle non-finite values.
Results may differ from a plain program's by a relative error of at most 0.0071.
Values may be sent and summed in bfloat16 or wider, within the bound.
A program may use at most 128 MiB of HBM per device.

v0:
```python
import jax
import jax.numpy as jnp
from jax import lax
from jax.sharding import PartitionSpec as P

SLOT_PER = 4


def divide_rows(summed, slot_totals):
    return (summed / slot_totals[:, None]).astype(jnp.bfloat16)


def shards(tokens, slot_params, expert_in, expert_out):
    logits = jnp.dot(tokens, slot_params, preferred_element_type=jnp.float32)
    local_peak = jnp.max(logits, axis=0)
    column_peak = lax.pmax(local_peak, ("wide", "narrow"))
    weights = jnp.exp(logits - column_peak)
    slot_totals = lax.psum(jnp.sum(weights, axis=0), ("wide", "narrow"))
    dispatch = weights.astype(jnp.bfloat16)
    slot_count = slot_params.shape[1]
    row_count = slot_count // lax.axis_size("wide")
    columns = dispatch
    partial_value = lax.psum_scatter(
        lax.dot_general(
            columns, tokens, (((0,), (0,)), ((), ())), preferred_element_type=jnp.float32
        ),
        "wide",
        scatter_dimension=0,
        tiled=True,
    )
    summed = lax.psum(partial_value, "narrow")
    owned_totals = lax.dynamic_slice_in_dim(
        slot_totals, lax.axis_index("wide") * row_count, row_count
    )
    slot_in = divide_rows(summed, owned_totals)
    slot_stack = slot_in.reshape(expert_in.shape[0], SLOT_PER, slot_in.shape[1])
    hidden = jax.nn.gelu(
        jnp.einsum("esd,edh->esh", slot_stack, expert_in, preferred_element_type=jnp.float32)
    ).astype(jnp.bfloat16)
    expert_sum = jnp.einsum("esh,ehd->esd", hidden, expert_out, preferred_element_type=jnp.float32)
    expert_sum = expert_sum.reshape(-1, expert_sum.shape[2])
    mixing = jax.nn.softmax(logits, axis=1).astype(jnp.bfloat16)
    whole_rows = lax.psum(expert_sum, "narrow").astype(jnp.bfloat16)
    columns = mixing
    mixed = jnp.dot(
        columns,
        lax.all_gather(whole_rows, "wide", axis=0, tiled=True),
        preferred_element_type=jnp.float32,
    )
    return mixed.astype(jnp.bfloat16)


def solution(mesh):
    return jax.shard_map(
        shards,
        mesh=mesh,
        in_specs=(
            P(("wide", "narrow"), None),
            P(),
            P("wide", None, "narrow"),
            P("wide", "narrow", None),
        ),
        out_specs=P(("wide", "narrow"), None),
        check_vma=False,
    )
```

profile of v0, /device:TPU:1, one launch (start us, length us, event | category | flops | bytes accessed | tf_op | source)
XLA Modules:
  0.0 312.3 jit_solution(13459068889585292751)
XLA Ops:
  6.5 0.0 copy-start
  6.5 0.0 reduce-scatter.2.cloned.1.call-start
  6.5 1.2 copy-done
  7.8 6.5 %fusion.26 = (f32[2048]{0:T(1024)S(1)}, f32[512]{0:T(512)S(1)}, f32[2048,512]{1,0:T(8,128)}) fusion(bf16[2048,1024]{1,0:T(8,128)(2,1)} %param.4, bf16[1024,512]{1,0:T(8,128)(2,1)S(1)} %copy-done), kind=kOutput, calls=%fused_computation.30 | convolution fusion | flops 2149578240 | bytes 9447424 | tf_op jit(solution)/shard_map/dot_general | solution.py:14
  14.2 68.6 %pmax.7 = f32[512]{0:T(512)S(1)} all-reduce(f32[512]{0:T(512)S(1)} %get-tuple-element.8), channel_id=1, replica_groups=mesh['wide'=32,'narrow'=4] {'wide','narrow'}, use_global_device_ids=true, to_apply=%region_3.0 | all-reduce | flops 512 | bytes 4096 | tf_op jit(solution)/shard_map/pmax | solution.py:16
  82.8 7.2 %fusion.3 = f32[512,1024]{1,0:T(8,128)} fusion(bf16[2048,1024]{1,0:T(8,128)(2,1)} %param.4, f32[2048,512]{1,0:T(8,128)} %get-tuple-element.9, f32[512]{0:T(512)S(1)} %pmax.7), kind=kOutput, calls=%fused_computation.7 | convolution fusion | flops 2149580800 | bytes 10487808 | tf_op jit(solution)/shard_map/dot_general | solution.py:24
  90.0 0.0 reduce-scatter.2.cloned.1.call-update
  90.0 0.0 all-reduce.2.cloned.1.call-start
  90.1 73.9 %reduce-scatter.2.cloned.1.call-done = f32[16,1024]{1,0:T(8,128)} async-done(((f32[512,1024]{1,0:T(8,128)}), f32[16,1024]{1,0:T(8,128)}) %reduce-scatter.2.cloned.1.call-update) | async-done | bytes 65552 | tf_op jit(solution)/shard_map/reduce_scatter | solution.py:23
  163.9 0.0 all-reduce.2.cloned.1.call-update
  164.0 0.0 all-gather.2.cloned.1.call-start
  164.0 3.1 %fusion = (f32[2048]{0:T(1024)S(1)}, f32[512]{0:T(512)S(1)}) fusion(f32[2048,512]{1,0:T(8,128)} %get-tuple-element.9, f32[2048]{0:T(1024)S(1)} %get-tuple-element.7, f32[512]{0:T(512)S(1)} %pmax.7), kind=kLoop, calls=%fused_computation.4 | loop fusion | flops 4191744 | bytes 4214784 | tf_op jit(solution)/shard_map/reduce_sum | solution.py:42
  167.2 66.0 %psum.22 = f32[512]{0:T(512)S(1)} all-reduce(f32[512]{0:T(512)S(1)} %get-tuple-element.6), channel_id=1, replica_groups=mesh['wide'=32,'narrow'=4] {'wide','narrow'}, use_global_device_ids=true, to_apply=%region_7.0 | all-reduce | flops 512 | bytes 4096 | tf_op jit(solution)/shard_map/psum | solution.py:18
  233.2 0.1 dynamic_slice.3
  233.3 0.0 all-reduce.2.cloned.1.call-done
  233.3 0.9 divide_convert_fusion.2
  234.2 8.0 %fusion.16 = f32[4,4,1024]{2,1,0:T(4,128)S(1)} fusion(bf16[4,1024,1024]{2,1,0:T(8,128)(2,1)} %param.7, bf16[4,4,1024]{2,1,0:T(4,128)(2,1)S(1)} %reshape.10, bf16[4,1024,1024]{2,1,0:T(8,128)(2,1)} %param.6), kind=kOutput, calls=%fused_computation.21 | convolution fusion | flops 67256320 | bytes 16875520 | tf_op jit(solution)/shard_map/esh,ehd->esd/dot_general | solution.py:40
  242.3 12.6 %psum.23 = bf16[16,1024]{1,0:T(8,128)(2,1)} all-reduce(f32[16,1024]{1,0:T(8,128)S(1)} %reshape.11), channel_id=1, replica_groups=mesh['wide'=32,'narrow'=4] {'narrow'}, use_global_device_ids=true, to_apply=%region_8.0 | all-reduce | flops 16384 | bytes 98304 | tf_op jit(solution)/shard_map/psum | solution.py:43
  254.9 0.0 all-gather.2.cloned.1.call-update
  254.9 43.9 %all-gather.2.cloned.1.call-done = bf16[512,1024]{1,0:T(8,128)(2,1)} async-done(((bf16[16,1024]{1,0:T(8,128)(2,1)}), bf16[512,1024]{1,0:T(8,128)(2,1)}) %all-gather.2.cloned.1.call-update) | async-done | bytes 1048592 | tf_op jit(solution)/shard_map/all_gather | solution.py:47
  298.7 7.0 %convolution_convert_fusion = bf16[2048,1024]{1,0:T(8,128)(2,1)} fusion(bf16[512,1024]{1,0:T(8,128)(2,1)} %all-gather.2.cloned.1.call-done, f32[2048,512]{1,0:T(8,128)} %get-tuple-element.9, f32[2048]{0:T(1024)S(1)} %get-tuple-element.5, f32[2048]{0:T(1024)S(1)} %get-tuple-element.7), kind=kOutput, calls=%fused_computation.3 | convolution fusion | flops 2152726528 | bytes 9453568 | tf_op jit(solution)/shard_map/dot_general | solution.py:45
  (2 shorter events, 0.1 us)
Async XLA Ops:
  6.5 1.2 copy-start
  6.5 157.4 %reduce-scatter.2.cloned.1.call-start = ((), (), s32[]{:S(2)}) async-start(), calls=%async_computation.1 | async-start | bytes 2162688 | tf_op jit(solution)/shard_map/reduce_scatter | solution.py:23
  90.0 143.2 %all-reduce.2.cloned.1.call-start = ((), (), s32[]{:S(2)}) async-start(), calls=%async_computation.2 | async-start | bytes 131072 | tf_op jit(solution)/shard_map/psum | solution.py:31
  164.0 134.8 %all-gather.2.cloned.1.call-start = ((), (), s32[]{:S(2)}) async-start(), calls=%async_computation.3 | async-start | bytes 1081344 | tf_op jit(solution)/shard_map/all_gather | solution.py:47
Sparse Core Ops, SparseCore 0:
  90.2 73.7 reduce-scatter.1
  166.2 40.1 all-reduce.1
  255.0 43.6 all-gather.1
where the time goes:
time: 313 us; the launch traced here: 312 us
  blocking collectives  147 us (47%)
  waiting for transfers between devices  118 us (38%)
  matrix products  28.7 us (9%)
  between operations  13.1 us (4%)
  other arithmetic  4.06 us (1%)
    reduce_scatter x1, waiting for transfers between devices, shards(): lax.psum_scatter(lax.dot_general(columns, tokens, (((0,), (0,)), ((), ())...  73.9 us
    pmax x1, blocking collectives, shards(): column_peak = lax.pmax(local_peak, ('wide', 'narrow'))  68.6 us
    psum x1, blocking collectives, shards(): slot_totals = lax.psum(jnp.sum(weights, axis=0), ('wide', 'narrow'))  66 us
    all_gather x1, waiting for transfers between devices, shards(): lax.all_gather(whole_rows, 'wide', axis=0, tiled=True)  43.9 us
    psum x1, blocking collectives, shards(): whole_rows = lax.psum(expert_sum, 'narrow').astype(jnp.bfloat16)  12.6 us
    dot_general x1, matrix products, shards(): jnp.einsum('esh,ehd->esd', hidden, expert_out, preferred_element_type=jnp...  8.04 us
    dot_general x1, matrix products, shards(): lax.dot_general(columns, tokens, (((0,), (0,)), ((), ())), preferred_elem...  7.15 us
    dot_general x1, matrix products, shards(): jnp.dot(columns, lax.all_gather(whole_rows, 'wide', axis=0, tiled=True),...  7.05 us
  transfers between devices with their start and end apart: 3, of which 2 were waited for; matrix products, arithmetic and copies ran while one was open for 1% of the time, Pallas kernels for 0%

commit v1 on v0

--- a/solution.py
+++ b/solution.py
@@ -4,6 +4,18 @@
 from jax.sharding import PartitionSpec as P
 
 SLOT_PER = 4
+
+
+def gather_by_bits(x, axis, dim):
+    ways, here = (lax.axis_size(axis), lax.axis_index(axis))
+    grown, reach = (x, 1)
+    while reach < ways:
+        theirs = lax.ppermute(grown, axis, [(d, d ^ reach) for d in range(ways)])
+        mine_first = jnp.concatenate([grown, theirs], axis=dim)
+        theirs_first = jnp.concatenate([theirs, grown], axis=dim)
+        grown = jnp.where(here & reach == 0, mine_first, theirs_first)
+        reach = 2 * reach
+    return grown
 
 
 def divide_rows(summed, slot_totals):
@@ -43,9 +55,7 @@
     whole_rows = lax.psum(expert_sum, "narrow").astype(jnp.bfloat16)
     columns = mixing
     mixed = jnp.dot(
-        columns,
-        lax.all_gather(whole_rows, "wide", axis=0, tiled=True),
-        preferred_element_type=jnp.float32,
+        columns, gather_by_bits(whole_rows, "wide", 0), preferred_element_type=jnp.float32
     )
     return mixed.astype(jnp.bfloat16)
 

time: 313 us -> 303 us (0.968)
  waiting for transfers between devices: 118 us -> 94.8 us
  starting transfers between devices: 0.08 us -> 11.5 us
    all_gather x1 -> x0, waiting for transfers between devices: 43.9 us -> none  [shards(): lax.all_gather(whole_rows, 'wide', axis=0, tiled=True)]
    ppermute x0 -> x5, waiting for transfers between devices: none -> 20.9 us  [gather_by_bits(): theirs = lax.ppermute(grown, axis, [(d, d ^ reach) for d in range(ways)])]
    ppermute x0 -> x5, starting transfers between devices: none -> 11.4 us  [gather_by_bits(): theirs = lax.ppermute(grown, axis, [(d, d ^ reach) for d in range(ways)])]
  transfers between devices with their start and end apart: 3 -> 7, of which waited for: 2 -> 6; matrix products, arithmetic and copies ran while one was open for 1% -> 1% of each run, Pallas kernels for 0% -> 0%
where the time goes in v1:
time: 303 us; the launch traced here: 300 us
  blocking collectives  146 us (48%)
  waiting for transfers between devices  94.8 us (31%)
  matrix products  28.4 us (9%)
  between operations  13.5 us (4%)
  starting transfers between devices  11.5 us (4%)
  other arithmetic  4.29 us (1%)
    reduce_scatter x1, waiting for transfers between devices, shards(): lax.psum_scatter(lax.dot_general(columns, tokens, (((0,), (0,)), ((), ())...  73.9 us
    pmax x1, blocking collectives, shards(): column_peak = lax.pmax(local_peak, ('wide', 'narrow'))  68.6 us
    psum x1, blocking collectives, shards(): slot_totals = lax.psum(jnp.sum(weights, axis=0), ('wide', 'narrow'))  66 us
    ppermute x5, waiting for transfers between devices, gather_by_bits(): theirs = lax.ppermute(grown, axis, [(d, d ^ reach) for d in range(ways)])  20.9 us
    psum x1, blocking collectives, shards(): whole_rows = lax.psum(expert_sum, 'narrow').astype(jnp.bfloat16)  11.8 us
    ppermute x5, starting transfers between devices, gather_by_bits(): theirs = lax.ppermute(grown, axis, [(d, d ^ reach) for d in range(ways)])  11.4 us
    dot_general x1, matrix products, shards(): jnp.einsum('esh,ehd->esd', hidden, expert_out, preferred_element_type=jnp...  8.04 us
    dot_general x1, matrix products, shards(): lax.dot_general(columns, tokens, (((0,), (0,)), ((), ())), preferred_elem...  7.15 us
  transfers between devices with their start and end apart: 7, of which 6 were waited for; matrix products, arithmetic and copies ran while one was open for 1% of the time, Pallas kernels for 0%

profile of v1, /device:TPU:1, one launch (start us, length us, event | category | flops | bytes accessed | tf_op | source)
XLA Modules:
  0.0 300.2 jit_solution(7513175797798102541)
XLA Ops:
  6.5 0.0 copy-start
  6.5 0.0 reduce-scatter.2.cloned.1.call-start
  6.5 1.2 copy-done
  7.8 6.5 %fusion.33 = (f32[512]{0:T(512)S(1)}, f32[2048]{0:T(1024)S(1)}, f32[2048,512]{1,0:T(8,128)}) fusion(bf16[2048,1024]{1,0:T(8,128)(2,1)} %param.4, bf16[1024,512]{1,0:T(8,128)(2,1)S(1)} %copy-done), kind=kOutput, calls=%fused_computation.42 | convolution fusion | flops 2149578240 | bytes 9447424 | tf_op jit(solution)/shard_map/dot_general | solution.py:26
  14.2 68.6 %pmax.7 = f32[512]{0:T(512)S(1)} all-reduce(f32[512]{0:T(512)S(1)} %get-tuple-element.7), channel_id=1, replica_groups=mesh['wide'=32,'narrow'=4] {'wide','narrow'}, use_global_device_ids=true, to_apply=%region_3.0 | all-reduce | flops 512 | bytes 4096 | tf_op jit(solution)/shard_map/pmax | solution.py:28
  82.9 7.2 %fusion.3 = f32[512,1024]{1,0:T(8,128)} fusion(bf16[2048,1024]{1,0:T(8,128)(2,1)} %param.4, f32[2048,512]{1,0:T(8,128)} %get-tuple-element.9, f32[512]{0:T(512)S(1)} %pmax.7), kind=kOutput, calls=%fused_computation.7 | convolution fusion | flops 2149580800 | bytes 10487808 | tf_op jit(solution)/shard_map/dot_general | solution.py:36
  90.0 0.0 reduce-scatter.2.cloned.1.call-update
  90.0 0.0 all-reduce.2.cloned.1.call-start
  90.1 73.9 %reduce-scatter.2.cloned.1.call-done = f32[16,1024]{1,0:T(8,128)} async-done(((f32[512,1024]{1,0:T(8,128)}), f32[16,1024]{1,0:T(8,128)}) %reduce-scatter.2.cloned.1.call-update) | async-done | bytes 65552 | tf_op jit(solution)/shard_map/reduce_scatter | solution.py:35
  164.0 0.0 all-reduce.2.cloned.1.call-update
  164.0 3.2 %fusion.1 = (f32[512]{0:T(512)S(1)}, f32[2048]{0:T(1024)S(1)}) fusion(f32[2048,512]{1,0:T(8,128)} %get-tuple-element.9, f32[512]{0:T(512)S(1)} %pmax.7, f32[2048]{0:T(1024)S(1)} %get-tuple-element.8), kind=kLoop, calls=%fused_computation.5 | loop fusion | flops 4191744 | bytes 4214784 | tf_op jit(solution)/shard_map/reduce_sum | solution.py:30
  167.2 66.0 %psum.22 = f32[512]{0:T(512)S(1)} all-reduce(f32[512]{0:T(512)S(1)} %get-tuple-element.5), channel_id=1, replica_groups=mesh['wide'=32,'narrow'=4] {'wide','narrow'}, use_global_device_ids=true, to_apply=%region_7.0 | all-reduce | flops 512 | bytes 4096 | tf_op jit(solution)/shard_map/psum | solution.py:30
  233.2 0.1 dynamic_slice.3
  233.2 0.0 all-reduce.2.cloned.1.call-done
  233.2 0.9 divide_convert_fusion.2
  234.2 8.0 %fusion.22 = f32[4,4,1024]{2,1,0:T(4,128)S(1)} fusion(bf16[4,1024,1024]{2,1,0:T(8,128)(2,1)} %param.7, bf16[4,4,1024]{2,1,0:T(4,128)(2,1)S(1)} %reshape.10, bf16[4,1024,1024]{2,1,0:T(8,128)(2,1)} %param.6), kind=kOutput, calls=%fused_computation.32 | convolution fusion | flops 67256320 | bytes 16875520 | tf_op jit(solution)/shard_map/esh,ehd->esd/dot_general | solution.py:52
  242.3 11.8 %psum.23 = bf16[16,1024]{1,0:T(8,128)(2,1)S(1)} all-reduce(f32[16,1024]{1,0:T(8,128)S(1)} %reshape.11), channel_id=1, replica_groups=mesh['wide'=32,'narrow'=4] {'narrow'}, use_global_device_ids=true, to_apply=%region_8.0 | all-reduce | flops 16384 | bytes 98304 | tf_op jit(solution)/shard_map/psum | solution.py:55
  254.0 4.5 %collective-permute-start = (bf16[16,1024]{1,0:T(8,128)(2,1)S(1)}, bf16[16,1024]{1,0:T(8,128)(2,1)S(1)}, u32[]{:S(2)}, u32[]{:S(2)}) collective-permute-start(bf16[16,1024]{1,0:T(8,128)(2,1)S(1)} %psum.23), channel_id=1, source_target_pairs={{0,4},{4,0},{8,12},{12,8},{16,20},{20,16},{24,28},{28,24},{32,36},... | collective-permute-start | bytes 98312 | tf_op jit(solution)/shard_map/ppermute | solution.py:13
  258.5 0.9 collective-permute-done
  259.3 1.3 collective-permute-start.1
  260.6 1.9 collective-permute-done.1
  262.6 2.3 collective-permute-start.2
  264.9 3.1 %collective-permute-done.2 = bf16[64,1024]{1,0:T(8,128)(2,1)S(1)} collective-permute-done((bf16[64,1024]{1,0:T(8,128)(2,1)S(1)}, bf16[64,1024]{1,0:T(8,128)(2,1)S(1)}, u32[]{:S(2)}, u32[]{:S(2)}) %collective-permute-start.2) | collective-permute-done | bytes 131104 | tf_op jit(solution)/shard_map/ppermute | solution.py:13
  268.0 1.3 collective-permute-start.3
  269.3 4.0 %collective-permute-done.3 = bf16[128,1024]{1,0:T(8,128)(2,1)S(1)} collective-permute-done((bf16[128,1024]{1,0:T(8,128)(2,1)S(1)}, bf16[128,1024]{1,0:T(8,128)(2,1)S(1)}, u32[]{:S(2)}, u32[]{:S(2)}) %collective-permute-start.3) | collective-permute-done | bytes 262176 | tf_op jit(solution)/shard_map/ppermute | solution.py:13
  273.3 0.1 maximum_select_fusion.2
  273.5 2.0 collective-permute-start.4
  275.5 11.1 %collective-permute-done.4 = bf16[256,1024]{1,0:T(8,128)(2,1)S(1)} collective-permute-done((bf16[256,1024]{1,0:T(8,128)(2,1)S(1)}, bf16[256,1024]{1,0:T(8,128)(2,1)S(1)}, u32[]{:S(2)}, u32[]{:S(2)}) %collective-permute-start.4) | collective-permute-done | bytes 524320 | tf_op jit(solution)/shard_map/ppermute | solution.py:13
  286.6 6.8 %convolution_convert_fusion = bf16[2048,1024]{1,0:T(8,128)(2,1)} fusion(f32[2048,512]{1,0:T(8,128)} %get-tuple-element.9, f32[2048]{0:T(1024)S(1)} %get-tuple-element.6, f32[2048]{0:T(1024)S(1)} %get-tuple-element.8, bf16[256,1024]{1,0:T(8,128)(2,1)S(1)} %collective-permute-done.4, bf16[256,1024]{1,0:T(8,128)(2,1)S(1)} %maximum_select_fusion.2, pred[]{:T(512)S(6)} %eq.15), kind=kOutput, calls=%fused_computation.3 | convolution fusion | flops 2157445120 | bytes 9453569 | tf_op jit(solution)/shard_map/dot_general | solution.py:57
  (5 shorter events, 0.1 us)
Async XLA Ops:
  6.5 1.2 copy-start
  6.5 157.4 %reduce-scatter.2.cloned.1.call-start = ((), (), s32[]{:S(2)}) async-start(), calls=%async_computation.1 | async-start | bytes 2162688 | tf_op jit(solution)/shard_map/reduce_scatter | solution.py:35
  90.0 143.2 %all-reduce.2.cloned.1.call-start = ((), (), s32[]{:S(2)}) async-start(), calls=%async_computation.2 | async-start | bytes 131072 | tf_op jit(solution)/shard_map/psum | solution.py:43
  254.0 5.3 %collective-permute-start = (bf16[16,1024]{1,0:T(8,128)(2,1)S(1)}, bf16[16,1024]{1,0:T(8,128)(2,1)S(1)}, u32[]{:S(2)}, u32[]{:S(2)}) collective-permute-start(bf16[16,1024]{1,0:T(8,128)(2,1)S(1)} %psum.23), channel_id=1, source_target_pairs={{0,4},{4,0},{8,12},{12,8},{16,20},{20,16},{24,28},{28,24},{32,36},... | collective-permute-start | bytes 98312 | tf_op jit(solution)/shard_map/ppermute | solution.py:13
  259.3 3.2 %collective-permute-start.1 = (bf16[32,1024]{1,0:T(8,128)(2,1)S(1)}, bf16[32,1024]{1,0:T(8,128)(2,1)S(1)}, u32[]{:S(2)}, u32[]{:S(2)}) collective-permute-start(bf16[32,1024]{1,0:T(8,128)(2,1)S(1)} %maximum_select_fusion.5), channel_id=1, source_target_pairs={{0,8},{4,12},{8,0},{12,4},{16,24},{20,28},{24,16},{28,20},{32,40},... | collective-permute-start | bytes 196616 | tf_op jit(solution)/shard_map/ppermute | solution.py:13
  262.6 5.4 %collective-permute-start.2 = (bf16[64,1024]{1,0:T(8,128)(2,1)S(1)}, bf16[64,1024]{1,0:T(8,128)(2,1)S(1)}, u32[]{:S(2)}, u32[]{:S(2)}) collective-permute-start(bf16[64,1024]{1,0:T(8,128)(2,1)S(1)} %maximum_select_fusion.4), channel_id=1, source_target_pairs={{0,16},{4,20},{8,24},{12,28},{16,0},{20,4},{24,8},{28,12},{32,48},... | collective-permute-start | bytes 393224 | tf_op jit(solution)/shard_map/ppermute | solution.py:13
  268.0 5.3 %collective-permute-start.3 = (bf16[128,1024]{1,0:T(8,128)(2,1)S(1)}, bf16[128,1024]{1,0:T(8,128)(2,1)S(1)}, u32[]{:S(2)}, u32[]{:S(2)}) collective-permute-start(bf16[128,1024]{1,0:T(8,128)(2,1)S(1)} %maximum_select_fusion.3), channel_id=1, source_target_pairs={{0,32},{4,36},{8,40},{12,44},{16,48},{20,52},{24,56},{28,60},{32,0... | collective-permute-start | bytes 786440 | tf_op jit(solution)/shard_map/ppermute | solution.py:13
  273.5 13.1 %collective-permute-start.4 = (bf16[256,1024]{1,0:T(8,128)(2,1)S(1)}, bf16[256,1024]{1,0:T(8,128)(2,1)S(1)}, u32[]{:S(2)}, u32[]{:S(2)}) collective-permute-start(bf16[256,1024]{1,0:T(8,128)(2,1)S(1)} %maximum_select_fusion.2), channel_id=1, source_target_pairs={{0,64},{4,68},{8,72},{12,76},{16,80},{20,84},{24,88},{28,92},{32,9... | collective-permute-start | bytes 1572872 | tf_op jit(solution)/shard_map/ppermute | solution.py:13
Sparse Core Ops, SparseCore 0:
  90.1 73.7 reduce-scatter.1
  166.3 40.0 all-reduce.1
